TPU v7x, 256 devices: a whole 4x4x8 slice. The times are simulated.
256 devices in a mesh: grp: 8 (over y, z_hi), tp: 4 (over z_lo), ffn: 8 (over x, core).
Axes of the slice: x: 4, y: 4, z: 8 (z_hi: 2, z_lo: 4; z = z_hi * 4 + z_lo), core: 2. Of those that a mesh axis runs over, the one named last changes fastest.
Arguments:
- queries: bfloat16 [768, 8192], P('grp', 'tp'), may hold values from -320 to 320
- new_kv: bfloat16 [2, 768, 1024], P(None, 'grp', 'tp'), may hold values from -12 to 12
- kv_cache: bfloat16 [2, 8, 16384, 1024], P(None, 'grp', 'ffn', 'tp'), may hold values from -12 to 12
- lengths: int32 [8], P('grp'), may hold values from 1 to 96, as said below
- prefixes: int32 [8], P('grp'), may hold values from 0 to 16384, as said below
- resid: bfloat16 [768, 8192], P('grp', 'ffn'), may hold values from -0.29882812 to 0.29882812
- out_weight: bfloat16 [8192, 8192], P('tp', 'ffn'), may hold values from -0.0625 to 0.0625
- gain: bfloat16 [8192], P('ffn'), may hold values from 0.099609375 to 1.8984375
- gate_weight: bfloat16 [8192, 29568], P('ffn', ('grp', 'tp')), may hold values from -0.0625 to 0.0625
- up_weight: bfloat16 [8192, 29568], P('ffn', ('grp', 'tp')), may hold values from -0.0625 to 0.0625
- down_weight: bfloat16 [29568, 8192], P(('grp', 'tp'), 'ffn'), may hold values from -0.03125 to 0.03125
Outputs:
- layer_out: bfloat16 [768, 8192], P(('grp', 'tp'), 'ffn')
Inputs may be any that keep to these rules, and one draw needn't show every extreme that they name: `lengths`: some group has a full block of 96 live slots. `prefixes`: some group has all 16384 cached positions in use.
All inputs are finite; a program needn't handle non-finite values.
Results may differ from a plain program's by a relative error of at most 0.02.
Values may be sent and summed in bfloat16 or wider, within the bound.
A program may use at most 64 MiB of HBM per device.

v0:
```python
import math
import jax
import jax.numpy as jnp
from jax import lax
from jax.sharding import PartitionSpec as P

D = 8192
DH = 128
negative = -1e30


def merged(x, axis, combine):
    everything = jax.tree.map(lambda part: lax.all_gather(part, axis), x)
    leading = jax.tree.map(lambda part: part[0], everything)

    def hop(k, so_far):
        return combine(so_far, jax.tree.map(lambda part: part[k], everything))

    return lax.fori_loop(1, lax.axis_size(axis), hop, leading)


def combine_parts(first, second):
    top = jnp.maximum(first[0], second[0])
    left = jnp.exp(first[0] - top)
    right = jnp.exp(second[0] - top)
    total = first[1] * left + second[1] * right
    values = first[2] * left[..., None] + second[2] * right[..., None]
    return (top, total, values)


def body(
    queries,
    new_kv,
    kv_cache,
    lengths,
    prefixes,
    resid,
    out_weight,
    gain,
    gate_weight,
    up_weight,
    down_weight,
):
    span, qcols = queries.shape
    kcols = new_kv.shape[2]
    local_kv = kcols // DH
    group = qcols // DH // local_kv
    cache_len = kv_cache.shape[2]
    length = lengths[0]
    prefix = prefixes[0]
    width_index = lax.axis_index("ffn")
    shard_start = width_index * cache_len
    query_heads = (
        queries.reshape(span, local_kv, group, DH)
        .transpose(1, 2, 0, 3)
        .reshape(local_kv, group * span, DH)
    )
    row_pos = jnp.tile(jnp.arange(span, dtype=jnp.int32), group)
    inv_scale = 1.0 / math.sqrt(DH)

    def update(state, keys, values, valid):
        top, total, acc = state
        scores = (
            jnp.einsum("hrd,hkd->hrk", query_heads, keys, preferred_element_type=jnp.float32)
            * inv_scale
        )
        scores = jnp.where(valid[None], scores, negative)
        new_top = jnp.maximum(top, jnp.max(scores, axis=-1))
        probs = jnp.where(valid[None], jnp.exp(scores - new_top[..., None]), 0.0)
        factor = jnp.exp(top - new_top)
        total = total * factor + jnp.sum(probs, axis=-1)
        acc = acc * factor[..., None] + jnp.einsum(
            "hrk,hkd->hrd", probs, values.astype(jnp.float32)
        )
        return (new_top, total, acc)

    block = math.gcd(512, cache_len)
    blocks = cache_len // block
    cache_keys = kv_cache[0, 0].reshape(blocks, block, local_kv, DH).transpose(0, 2, 1, 3)
    cache_values = kv_cache[1, 0].reshape(blocks, block, local_kv, DH).transpose(0, 2, 1, 3)
    rows = group * span
    start_state = (
        jnp.full((local_kv, rows), negative, jnp.float32),
        jnp.zeros((local_kv, rows), jnp.float32),
        jnp.zeros((local_kv, rows, DH), jnp.float32),
    )

    def cache_step(state, items):
        keys, values, index = items
        positions = shard_start + index * block + jnp.arange(block, dtype=jnp.int32)
        valid = jnp.broadcast_to((positions < prefix)[None, :], (rows, block))
        return (update(state, keys, values, valid), None)

    state, unused = lax.scan(
        cache_step, start_state, (cache_keys, cache_values, jnp.arange(blocks, dtype=jnp.int32))
    )
    block_keys = new_kv[0].reshape(span, local_kv, DH).transpose(1, 0, 2)
    block_values = new_kv[1].reshape(span, local_kv, DH).transpose(1, 0, 2)
    slots = jnp.arange(span, dtype=jnp.int32)[None, :]
    new_valid = (slots < length) & (slots <= row_pos[:, None]) & (width_index == 0)
    state = update(state, block_keys, block_values, new_valid)
    top, total, acc = merged(state, "ffn", combine_parts)
    heads = acc / total[..., None]
    attn = (
        heads.reshape(local_kv, group, span, DH)
        .transpose(2, 0, 1, 3)
        .reshape(span, qcols)
        .astype(jnp.bfloat16)
    )
    partial_value = jnp.dot(attn, out_weight, preferred_element_type=jnp.float32)
    summed = lax.psum(partial_value, "tp")
    h1 = (summed + resid.astype(jnp.float32)).astype(jnp.bfloat16)
    all_rows = lax.all_gather(h1, "grp", axis=0, tiled=True)
    rows_f = all_rows.astype(jnp.float32)
    squares = jnp.sum(rows_f * rows_f, axis=1)
    scaled = (rows_f * gain.astype(jnp.float32)[None, :]).astype(jnp.bfloat16)
    gate = jnp.dot(scaled, gate_weight, preferred_element_type=jnp.float32)
    upper = jnp.dot(scaled, up_weight, preferred_element_type=jnp.float32)
    rows_here = span // lax.axis_size("tp")
    gate, upper, squares = lax.psum((gate, upper, squares), "ffn")
    inv_rms = lax.rsqrt(squares / D + 1e-06)
    hidden = (jax.nn.silu(gate * inv_rms[:, None]) * (upper * inv_rms[:, None])).astype(
        jnp.bfloat16
    )
    down_rows = lax.psum_scatter(
        jnp.dot(hidden, down_weight, preferred_element_type=jnp.float32),
        ("grp", "tp"),
        scatter_dimension=0,
        tiled=True,
    )
    row_start = lax.axis_index("tp") * rows_here
    own = lax.dynamic_slice_in_dim(h1, row_start, rows_here, 0)
    live = row_start + jnp.arange(rows_here, dtype=jnp.int32) < length
    return jnp.where(live[:, None], own.astype(jnp.float32) + down_rows, 0.0).astype(jnp.bfloat16)


def solution(mesh):
    return jax.shard_map(
        body,
        mesh=mesh,
        in_specs=(
            P("grp", "tp"),
            P(None, "grp", "tp"),
            P(None, "grp", "ffn", "tp"),
            P("grp"),
            P("grp"),
            P("grp", "ffn"),
            P("tp", "ffn"),
            P("ffn"),
            P("ffn", ("grp", "tp")),
            P("ffn", ("grp", "tp")),
            P(("grp", "tp"), "ffn"),
        ),
        out_specs=P(("grp", "tp"), "ffn"),
        check_vma=False,
    )
```

profile of v0, /device:TPU:2, one launch (start us, length us, event | category | flops | bytes accessed | tf_op | source)
XLA Modules:
  0.0 559.2 jit_solution(7451356754690004521)
XLA Ops:
  9.5 3.0 fusion.47
  13.9 2.1 reshape_squeeze.12
  16.0 28.8 %while.35 = (s32[]{:T(128)}, f32[2,768]{1,0:T(2,128)S(1)}, f32[2,768]{1,0:T(2,128)S(1)}, f32[2,768,128]{2,1,0:T(8,128)}, s32[4]{0:T(128)S(1)}, /*index=5*/s32[]{...) while((s32[]{:T(128)}, f32[2,768]{1,0:T(2,128)S(1)}, ...), condition=%wide.region_3.4_spmd.clone, body=%wide.region_0.3_spmd.clone.sunk | while | flops 412688896 | bytes 19368184 | solution.py:94
  45.4 2.5 convolution_add_fusion
  48.0 12.9 %all-gather.4 = f32[8,2,768]{2,1,0:T(2,128)S(1)} all-gather(f32[1,2,768]{2,1,0:T(2,128)S(1)} %get-tuple-element.336), channel_id=3, replica_groups=mesh['grp'=8,'tp'=4,'ffn'=8] {'ffn'}, dimensions={0}, use_global_device_ids=true | all-gather | bytes 55296 | tf_op jit(solution)/shard_map/all_gather | solution.py:13
  60.8 12.8 %all-gather.3 = f32[8,2,768]{2,1,0:T(2,128)S(1)} all-gather(f32[1,2,768]{2,1,0:T(2,128)S(1)} %bitcast.107), channel_id=2, replica_groups=mesh['grp'=8,'tp'=4,'ffn'=8] {'ffn'}, dimensions={0}, use_global_device_ids=true | all-gather | bytes 55296 | tf_op jit(solution)/shard_map/all_gather | solution.py:13
  73.6 20.0 %all-gather.10.cloned.1.call-done = f32[16,768,128]{2,1,0:T(8,128)} async-done(((f32[2,768,128]{2,1,0:T(8,128)}), f32[16,768,128]{2,1,0:T(8,128)}) %all-gather.10.cloned.1.call-update) | async-done | bytes 6291472 | tf_op jit(solution)/shard_map/all_gather | solution.py:13
  94.8 13.0 %while.34 = (s32[]{:T(128)}, f32[2,768]{1,0:T(2,128)S(1)}, f32[2,768]{1,0:T(2,128)S(1)}, f32[2,768,128]{2,1,0:T(8,128)S(1)}, f32[8,2,768]{2,1,0:T(2,128)S(1)}, /...) while((s32[]{:T(128)}, f32[2,768]{1,0:T(2,128)S(1)}, ...), condition=%wide.region_7.8_spmd, body=%wide.region_6.7_spmd.sunk | while | flops 599045 | bytes 2420879 | solution.py:19
  94.9 1.8 fusion.65
  96.7 1.8 fusion.65
  98.6 1.8 fusion.65
  100.5 1.8 fusion.65
  102.3 1.8 fusion.65
  104.2 1.8 fusion.65
  106.0 1.8 fusion.65
  108.3 3.8 fusion.32
  112.2 52.0 %all-reduce.4.cloned.1.call-done = f32[96,1024]{1,0:T(8,128)} async-done(((f32[96,1024]{1,0:T(8,128)}), f32[96,1024]{1,0:T(8,128)}) %all-reduce.4.cloned.1.call-update) | async-done | bytes 393232 | tf_op jit(solution)/shard_map/psum | solution.py:111
  165.9 69.0 %all-gather.8.cloned.1.call-done = bf16[768,1024]{1,0:T(8,128)(2,1)} async-done(((bf16[96,1024]{1,0:T(8,128)(2,1)}), bf16[768,1024]{1,0:T(8,128)(2,1)}) %all-gather.8.cloned.1.call-update) | async-done | bytes 1572880 | tf_op jit(solution)/shard_map/all_gather | solution.py:113
  235.0 5.4 fusion.26
  240.4 3.3 fusion.28
  244.1 10.0 %psum.30 = f32[768]{0:T(1024)S(1)} all-reduce(f32[768]{0:T(1024)S(1)} %fusion.24), channel_id=1, replica_groups=mesh['grp'=8,'tp'=4,'ffn'=8] {'ffn'}, use_global_device_ids=true, to_apply=%region_11.12 | all-reduce | flops 768 | bytes 6144 | tf_op jit(solution)/shard_map/psum | solution.py:120
  254.2 68.5 %all-reduce.6.cloned.1.call-done = (f32[768,924]{0,1:T(8,128)}, f32[768,924]{0,1:T(8,128)}) async-done(((f32[768,924]{0,1:T(8,128)}, f32[768,924]{0,1:T(8,128)}), (f32[768,924]{0,1:T(8,128)}, f32[768,924]{0,1:T(8,128)})) %all-reduce.6.cloned.1.call-update) | async-done | bytes 5677072 | tf_op jit(solution)/shard_map/psum | solution.py:120
  322.7 6.2 %fusion.25 = f32[768,1024]{1,0:T(8,128)} fusion(bf16[924,1024]{1,0:T(8,128)(2,1)S(1)} %copy-done, f32[768,924]{0,1:T(8,128)} %get-tuple-element.328, f32[768,924]{0,1:T(8,128)} %get-tuple-element.329, f32[768]{0:T(1024)S(1)} %add_rsqrt_fusion), kind=kOutput, calls=%fused_computation.42 | convolution fusion | flops 1459003392 | bytes 10718208 | tf_op jit(solution)/shard_map/dot_general | solution.py:126
  329.0 222.1 %reduce-scatter.2.cloned.1.call-done = f32[24,1024]{1,0:T(8,128)} async-done(((f32[768,1024]{1,0:T(8,128)}), f32[24,1024]{1,0:T(8,128)}) %reduce-scatter.2.cloned.1.call-update) | async-done | bytes 98320 | tf_op jit(solution)/shard_map/reduce_scatter | solution.py:125
  (108 shorter events, 35.9 us)
Async XLA Ops:
  6.5 316.1 %copy-start = (bf16[924,1024]{1,0:T(8,128)(2,1)S(1)}, bf16[924,1024]{1,0:T(8,128)(2,1)}, u32[]{:S(2)}) copy-start(bf16[924,1024]{1,0:T(8,128)(2,1)} %param.25) | copy-start | bytes 5677060
  6.5 87.1 %all-gather.10.cloned.1.call-start = ((), (), s32[]{:S(2)}) async-start(), calls=%async_computation.4 | async-start | bytes 7077888 | tf_op jit(solution)/shard_map/all_gather | solution.py:13
  19.3 1.5 copy-start.2
  22.3 0.9 copy-start.3
  26.5 1.5 copy-start.2
  29.5 0.9 copy-start.3
  33.7 1.5 copy-start.2
  36.7 0.9 copy-start.3
  40.9 1.5 copy-start.2
  43.9 0.9 copy-start.3
  47.9 116.2 %all-reduce.4.cloned.1.call-start = ((), (), s32[]{:S(2)}) async-start(), calls=%async_computation.1 | async-start | bytes 786432 | tf_op jit(solution)/shard_map/psum | solution.py:111
  108.3 55.9 %copy-start.4 = (bf16[96,1024]{1,0:T(8,128)(2,1)S(1)}, bf16[96,1024]{1,0:T(8,128)(2,1)}, u32[]{:S(2)}) copy-start(bf16[96,1024]{1,0:T(8,128)(2,1)} %param.20) | copy-start | bytes 589828
  108.3 57.6 %copy-start.5 = (bf16[1024]{0:T(1024)(128)(2,1)S(1)}, bf16[1024]{0:T(1024)(128)(2,1)}, u32[]{:S(2)}) copy-start(bf16[1024]{0:T(1024)(128)(2,1)} %param.22) | copy-start | bytes 6148
  112.1 122.8 %all-gather.8.cloned.1.call-start = ((), (), s32[]{:S(2)}) async-start(), calls=%async_computation.2 | async-start | bytes 1769472 | tf_op jit(solution)/shard_map/all_gather | solution.py:113
  165.9 156.8 %all-reduce.6.cloned.1.call-start = ((), (), s32[]{:S(2)}) async-start(), calls=%async_computation.5 | async-start | bytes 11403264 | tf_op jit(solution)/shard_map/psum | solution.py:120
  235.0 5.4 copy-start.1
  235.0 5.4 copy-start.6
  243.7 307.4 %reduce-scatter.2.cloned.1.call-start = ((), (), s32[]{:S(2)}) async-start(), calls=%async_computation.3 | async-start | bytes 3244032 | tf_op jit(solution)/shard_map/reduce_scatter | solution.py:125
Sparse Core Ops, SparseCore 0:
  48.0 45.5 all-gather.9
  112.2 51.8 all-reduce.3
  167.1 67.8 all-gather.7
  243.8 78.8 all-reduce.5
  329.1 221.9 reduce-scatter.1
where the time goes:
time: 560 us; the launch traced here: 559 us
  waiting for transfers between devices  432 us (77%)
  blocking collectives  35.7 us (6%)
  matrix products  30 us (5%)
  other arithmetic  23.3 us (4%)
  local copies, waits for them, and re-layouts  21.3 us (4%)
  between operations  14.1 us (3%)
    reduce_scatter x1, waiting for transfers between devices, body(): lax.psum_scatter(jnp.dot(hidden, down_weight, preferred_element_type=jnp....  222 us
    all_gather x1, waiting for transfers between devices, body(): all_rows = lax.all_gather(h1, 'grp', axis=0, tiled=True)  69 us
    psum x1, waiting for transfers between devices, body(): gate, upper, squares = lax.psum((gate, upper, squares), 'ffn')  68.5 us
    psum x1, waiting for transfers between devices, body(): summed = lax.psum(partial_value, 'tp')  52 us
    all_gather x2, blocking collectives, merged(): everything = jax.tree.map(lambda part: lax.all_gather(part, axis), x)  25.6 us
    all_gather x1, waiting for transfers between devices, merged(): everything = jax.tree.map(lambda part: lax.all_gather(part, axis), x)  20 us
    add x7, other arithmetic, combine_parts(): values = first[2] * left[..., None] + second[2] * right[..., None]  12.6 us
  transfers between devices with their start and end apart: 5, of which 5 were waited for; matrix products, arithmetic and copies ran while one was open for 0% of the time, Pallas kernels for 0%

commit v1 on v0

--- a/solution.py
+++ b/solution.py
@@ -110,7 +110,8 @@
     partial_value = jnp.dot(attn, out_weight, preferred_element_type=jnp.float32)
     summed = lax.psum(partial_value, "tp")
     h1 = (summed + resid.astype(jnp.float32)).astype(jnp.bfloat16)
-    all_rows = lax.all_gather(h1, "grp", axis=0, tiled=True)
+    sent = jnp.stack([h1] * lax.axis_size("grp"))
+    all_rows = jnp.concatenate(lax.all_to_all(sent, "grp", 0, 0), axis=0)
     rows_f = all_rows.astype(jnp.float32)
     squares = jnp.sum(rows_f * rows_f, axis=1)
     scaled = (rows_f * gain.astype(jnp.float32)[None, :]).astype(jnp.bfloat16)

time: 560 us -> 538 us (0.961)
  waiting for transfers between devices: 432 us -> 402 us
  starting transfers between devices: 0.17 us -> 6.94 us
    all_gather x1 -> x0, waiting for transfers between devices: 69 us -> none  [body(): all_rows = lax.all_gather(h1, 'grp', axis=0, tiled=True)]
    all_to_all x0 -> x1, waiting for transfers between devices: none -> 35.1 us  [body(): all_rows = jnp.concatenate(lax.all_to_all(sent, 'grp', 0, 0), axis=0)]
    all_to_all x0 -> x1, starting transfers between devices: none -> 6.81 us  [body(): all_rows = jnp.concatenate(lax.all_to_all(sent, 'grp', 0, 0), axis=0)]
where the time goes in v1:
time: 538 us; the launch traced here: 537 us
  waiting for transfers between devices  402 us (75%)
  blocking collectives  35.6 us (7%)
  matrix products  27.8 us (5%)
  local copies, waits for them, and re-layouts  24.5 us (5%)
  other arithmetic  23 us (4%)
  between operations  14.1 us (3%)
  starting transfers between devices  6.94 us (1%)
    reduce_scatter x1, waiting for transfers between devices, body(): lax.psum_scatter(jnp.dot(hidden, down_weight, preferred_element_type=jnp....  222 us
    psum x1, waiting for transfers between devices, body(): gate, upper, squares = lax.psum((gate, upper, squares), 'ffn')  72.6 us
    psum x1, waiting for transfers between devices, body(): summed = lax.psum(partial_value, 'tp')  52 us
    all_to_all x1, waiting for transfers between devices, body(): all_rows = jnp.concatenate(lax.all_to_all(sent, 'grp', 0, 0), axis=0)  35.1 us
    all_gather x2, blocking collectives, merged(): everything = jax.tree.map(lambda part: lax.all_gather(part, axis), x)  25.6 us
    all_gather x1, waiting for transfers between devices, merged(): everything = jax.tree.map(lambda part: lax.all_gather(part, axis), x)  20 us
    add x7, other arithmetic, combine_parts(): values = first[2] * left[..., None] + second[2] * right[..., None]  12.6 us
  transfers between devices with their start and end apart: 5, of which 5 were waited for; matrix products, arithmetic and copies ran while one was open for 0% of the time, Pallas kernels for 0%

profile of v1, /device:TPU:2, one launch (start us, length us, event | category | flops | bytes accessed | tf_op | source)
XLA Modules:
  0.0 536.7 jit_solution(15967455581443982343)
XLA Ops:
  9.5 3.0 fusion.42
  13.9 2.1 reshape_squeeze.12
  16.0 28.8 %while.35 = (s32[]{:T(128)}, f32[2,768]{1,0:T(2,128)S(1)}, f32[2,768]{1,0:T(2,128)S(1)}, f32[2,768,128]{2,1,0:T(8,128)}, s32[4]{0:T(128)S(1)}, /*index=5*/s32[]{...) while((s32[]{:T(128)}, f32[2,768]{1,0:T(2,128)S(1)}, ...), condition=%wide.region_3.4_spmd.clone, body=%wide.region_0.3_spmd.clone.sunk | while | flops 412688896 | bytes 19368184 | solution.py:94
  45.4 2.5 convolution_add_fusion
  48.0 12.9 %all-gather.4 = f32[8,2,768]{2,1,0:T(2,128)S(1)} all-gather(f32[1,2,768]{2,1,0:T(2,128)S(1)} %get-tuple-element.346), channel_id=3, replica_groups=mesh['grp'=8,'tp'=4,'ffn'=8] {'ffn'}, dimensions={0}, use_global_device_ids=true | all-gather | bytes 55296 | tf_op jit(solution)/shard_map/all_gather | solution.py:13
  60.8 12.8 %all-gather.3 = f32[8,2,768]{2,1,0:T(2,128)S(1)} all-gather(f32[1,2,768]{2,1,0:T(2,128)S(1)} %bitcast.113), channel_id=2, replica_groups=mesh['grp'=8,'tp'=4,'ffn'=8] {'ffn'}, dimensions={0}, use_global_device_ids=true | all-gather | bytes 55296 | tf_op jit(solution)/shard_map/all_gather | solution.py:13
  73.6 20.0 %all-gather.7.cloned.1.call-done = f32[16,768,128]{2,1,0:T(8,128)} async-done(((f32[2,768,128]{2,1,0:T(8,128)}), f32[16,768,128]{2,1,0:T(8,128)}) %all-gather.7.cloned.1.call-update) | async-done | bytes 6291472 | tf_op jit(solution)/shard_map/all_gather | solution.py:13
  94.8 13.0 %while.34 = (s32[]{:T(128)}, f32[2,768]{1,0:T(2,128)S(1)}, f32[2,768]{1,0:T(2,128)S(1)}, f32[2,768,128]{2,1,0:T(8,128)S(1)}, f32[8,2,768]{2,1,0:T(2,128)S(1)}, /...) while((s32[]{:T(128)}, f32[2,768]{1,0:T(2,128)S(1)}, ...), condition=%wide.region_7.8_spmd, body=%wide.region_6.7_spmd.sunk | while | flops 599045 | bytes 2420879 | solution.py:19
  94.9 1.8 fusion.64
  96.7 1.8 fusion.64
  98.6 1.8 fusion.64
  100.5 1.8 fusion.64
  102.3 1.8 fusion.64
  104.2 1.8 fusion.64
  108.3 3.8 fusion.27
  112.1 52.0 %all-reduce.4.cloned.1.call-done = f32[96,1024]{1,0:T(8,128)} async-done(((f32[96,1024]{1,0:T(8,128)}), f32[96,1024]{1,0:T(8,128)}) %all-reduce.4.cloned.1.call-update) | async-done | bytes 393232 | tf_op jit(solution)/shard_map/psum | solution.py:111
  167.2 6.8 %all-to-all-start = ((bf16[8,96,1024]{2,1,0:T(8,128)(2,1)}), bf16[8,96,1024]{2,1,0:T(8,128)(2,1)S(1)}, u32[]{:S(2)}, u32[]{:S(2)}) async-start(bf16[8,96,1024]{2,1,0:T(8,128)(2,1)} %stack.2), calls=%async_computation | async-start | bytes 3145728 | tf_op jit(solution)/shard_map/all_to_all | solution.py:114
  174.1 35.1 %all-to-all-done = bf16[8,96,1024]{2,1,0:T(8,128)(2,1)S(1)} async-done(((bf16[8,96,1024]{2,1,0:T(8,128)(2,1)}), bf16[8,96,1024]{2,1,0:T(8,128)(2,1)S(1)}, u32[]{:S(2)}, u32[]{:S(2)}) %all-to-all-start) | async-done | bytes 1572896 | tf_op jit(solution)/shard_map/all_to_all | solution.py:114
  210.7 3.2 fusion.46
  213.9 3.3 fusion.45
  217.7 10.0 %psum.30 = f32[768]{0:T(1024)S(1)} all-reduce(f32[768]{0:T(1024)S(1)} %reduce_sum.31), channel_id=1, replica_groups=mesh['grp'=8,'tp'=4,'ffn'=8] {'ffn'}, use_global_device_ids=true, to_apply=%region_11.12 | all-reduce | flops 768 | bytes 6144 | tf_op jit(solution)/shard_map/psum | solution.py:121
  227.7 72.6 %all-reduce.6.cloned.1.call-done = (f32[768,924]{0,1:T(8,128)}, f32[768,924]{0,1:T(8,128)}) async-done(((f32[768,924]{0,1:T(8,128)}, f32[768,924]{0,1:T(8,128)}), (f32[768,924]{0,1:T(8,128)}, f32[768,924]{0,1:T(8,128)})) %all-reduce.6.cloned.1.call-update) | async-done | bytes 5677072 | tf_op jit(solution)/shard_map/psum | solution.py:121
  300.4 6.2 %fusion.24 = f32[768,1024]{1,0:T(8,128)} fusion(bf16[924,1024]{1,0:T(8,128)(2,1)S(1)} %copy-done, f32[768,924]{0,1:T(8,128)} %get-tuple-element.338, f32[768,924]{0,1:T(8,128)} %get-tuple-element.339, f32[768]{0:T(1024)S(1)} %add_rsqrt_fusion), kind=kOutput, calls=%fused_computation.41 | convolution fusion | flops 1459003392 | bytes 10718208 | tf_op jit(solution)/shard_map/dot_general | solution.py:127
  306.7 221.9 %reduce-scatter.2.cloned.1.call-done = f32[24,1024]{1,0:T(8,128)} async-done(((f32[768,1024]{1,0:T(8,128)}), f32[24,1024]{1,0:T(8,128)}) %reduce-scatter.2.cloned.1.call-update) | async-done | bytes 98320 | tf_op jit(solution)/shard_map/reduce_scatter | solution.py:126
  (112 shorter events, 40.5 us)
Async XLA Ops:
  6.5 293.8 %copy-start = (bf16[924,1024]{1,0:T(8,128)(2,1)S(1)}, bf16[924,1024]{1,0:T(8,128)(2,1)}, u32[]{:S(2)}) copy-start(bf16[924,1024]{1,0:T(8,128)(2,1)} %param.25) | copy-start | bytes 5677060
  6.5 87.1 %all-gather.7.cloned.1.call-start = ((), (), s32[]{:S(2)}) async-start(), calls=%async_computation.4 | async-start | bytes 7077888 | tf_op jit(solution)/shard_map/all_gather | solution.py:13
  19.3 1.5 copy-start.2
  22.3 0.9 copy-start.3
  26.5 1.5 copy-start.2
  29.5 0.9 copy-start.3
  33.7 1.5 copy-start.2
  36.7 0.9 copy-start.3
  40.9 1.5 copy-start.2
  43.9 0.9 copy-start.3
  47.9 116.2 %all-reduce.4.cloned.1.call-start = ((), (), s32[]{:S(2)}) async-start(), calls=%async_computation.2 | async-start | bytes 786432 | tf_op jit(solution)/shard_map/psum | solution.py:111
  108.3 55.9 %copy-start.4 = (bf16[96,1024]{1,0:T(8,128)(2,1)S(1)}, bf16[96,1024]{1,0:T(8,128)(2,1)}, u32[]{:S(2)}) copy-start(bf16[96,1024]{1,0:T(8,128)(2,1)} %param.20) | copy-start | bytes 589828
  112.1 61.9 %copy-start.5 = (bf16[1024]{0:T(1024)(128)(2,1)S(1)}, bf16[1024]{0:T(1024)(128)(2,1)}, u32[]{:S(2)}) copy-start(bf16[1024]{0:T(1024)(128)(2,1)} %param.22) | copy-start | bytes 6148
  165.2 0.7 copy-start.1
  167.2 41.9 %all-to-all-start = ((bf16[8,96,1024]{2,1,0:T(8,128)(2,1)}), bf16[8,96,1024]{2,1,0:T(8,128)(2,1)S(1)}, u32[]{:S(2)}, u32[]{:S(2)}) async-start(bf16[8,96,1024]{2,1,0:T(8,128)(2,1)} %stack.2), calls=%async_computation | async-start | bytes 3145728 | tf_op jit(solution)/shard_map/all_to_all | solution.py:114
  174.0 126.4 %all-reduce.6.cloned.1.call-start = ((), (), s32[]{:S(2)}) async-start(), calls=%async_computation.5 | async-start | bytes 11403264 | tf_op jit(solution)/shard_map/psum | solution.py:121
  209.1 1.5 copy-start.6
  210.7 3.2 copy-start.7
  217.2 311.4 %reduce-scatter.2.cloned.1.call-start = ((), (), s32[]{:S(2)}) async-start(), calls=%async_computation.3 | async-start | bytes 3244032 | tf_op jit(solution)/shard_map/reduce_scatter | solution.py:126
Sparse Core Ops, SparseCore 0:
  48.0 45.5 all-gather.6
  112.2 51.8 all-reduce.3
  217.3 82.9 all-reduce.5
  306.8 221.7 reduce-scatter.1
